TPU v7x, 32 devices: a whole 2x2x4 slice. The times are simulated.
32 devices in a mesh: groups: 2 (over x), seq: 16 (over z, y, core).
Axes of the slice: x: 2, y: 2, z: 4, core: 2. Of those that a mesh axis runs over, the one named last changes fastest.
Arguments:
- query_rows: bfloat16 [8192, 1024], P(('groups', 'seq')), parts along dimension 0, may hold values from -25 to 25
- key_rows: bfloat16 [8192, 1024], P(('groups', 'seq')), parts along dimension 0, may hold values from -18 to 18
- value_rows: bfloat16 [8192, 1024], P(('groups', 'seq')), parts along dimension 0, may hold values from -18 to 18
- segment_ids: int32 [8192], P(('groups', 'seq')), parts along dimension 0, may hold values from 0 to 2, never falling along the last dimension, each value on 1 to 2560 neighbouring positions
- out_weight: bfloat16 [1024, 1024], replicated, may hold values from -0.1875 to 0.1875
Outputs:
- attended: bfloat16 [8192, 1024], P(('groups', 'seq')), parts along dimension 0
There are 2 independent parts, one for each index of `groups`. A program takes and returns all parts, laid end to end along the dimension named above; an argument that names none is the same for every part. Nothing has to cross between parts.
Inputs may be any that keep to these rules, and one draw needn't show every extreme that they name: `segment_ids`: ids never fall along the sequence; there are three transcripts, one of exactly 2560 tokens.
All inputs are finite; a program needn't handle non-finite values.
Results may differ from a plain program's by a relative error of at most 0.0051.
Values may be sent and summed in bfloat16 or wider, within the bound.
A program may use at most 128 MiB of HBM per device.

v0:
```python
import functools
import jax
import jax.numpy as jnp
from jax import lax
from jax.experimental import pallas as pl
from jax.experimental.pallas import tpu as pltpu
from jax.sharding import PartitionSpec as P

H = 16
DH = 64
TILE = 128
LANES = 128
MIN_ROWS = 16
BIG = 2.0**100


def flip(index, mask):
    bit = 0
    while (1 << bit) <= mask:
        if mask & (1 << bit):
            index = index + (1 - 2 * ((index // (1 << bit)) % 2)) * (1 << bit)
        bit += 1
    return index


def level_plan(level):
    rows = max(TILE >> (level - 1), MIN_ROWS)
    shared = max(0, level - 4)
    low = max(1, shared)
    masks = [(1 << (level - 1)) + (c << low) for c in range(1 << max(0, level - 1 - low))]
    return rows, shared, masks, shared == 0 and level > 1


def halve(source):
    rows = source.shape[0]
    row = lax.broadcasted_iota(jnp.int32, (rows // 2, rows), 0)
    col = lax.broadcasted_iota(jnp.int32, (rows // 2, rows), 1)
    pick = jnp.where(col // 2 == row, 0.5, 0.0).astype(jnp.bfloat16)
    return jnp.dot(pick, source, preferred_element_type=jnp.float32).astype(jnp.bfloat16)


def attend(devices, q_ref, k_ref, v_ref, seg_ref, w_hbm, out_ref, kv, left, right, queries,
           query_seg, largest, total, context, w_vmem, w_sem, halo_send, halo_recv, *rest):
    levels = devices.bit_length() - 1
    pieces = rest[:levels]
    blocks = rest[levels : 2 * levels]
    send, recv, fsend, frecv = rest[2 * levels : 2 * levels + 4]
    joins = rest[2 * levels + 4 : -2] if levels > 4 else ()
    if levels > 4:
        jsend, jrecv = rest[-2:]
    me = lax.axis_index("seq")
    width = q_ref.shape[1]
    pairs = width // LANES
    plans = [level_plan(level) for level in range(1, levels + 1)]

    def to(mask):
        return {"seq": flip(me, mask)}

    before = (me + devices - 1) % devices
    after = (me + 1) % devices
    masks = {1}
    for _, _, some, _ in plans:
        masks.update(some)
    for level in range(5, levels + 1):
        masks.add(1 << (level - 5))
    masks = sorted(masks)
    barrier = pltpu.get_barrier_semaphore()
    for mask in masks:
        pl.semaphore_signal(barrier, inc=1, device_id=to(mask),
                            device_id_type=pl.DeviceIdType.MESH)
    for target in (before, after):
        pl.semaphore_signal(barrier, inc=1, device_id={"seq": target},
                            device_id_type=pl.DeviceIdType.MESH)

    w_copy = pltpu.make_async_copy(w_hbm, w_vmem, w_sem)
    w_copy.start()

    tokens = q_ref.shape[0]
    seg = seg_ref[...]
    first = jnp.sum(jnp.where(seg < 1, 1.0, 0.0), axis=1, keepdims=True)
    second = jnp.sum(jnp.where(seg < 2, 1.0, 0.0), axis=1, keepdims=True)
    row = lax.broadcasted_iota(jnp.int32, (tokens, LANES), 0).astype(jnp.float32)
    lane = lax.broadcasted_iota(jnp.int32, (tokens, LANES), 1).astype(jnp.float32)
    row_seg = jnp.where(row >= first, 1.0, 0.0) + jnp.where(row >= second, 1.0, 0.0)
    kv[:, :width] = k_ref[...]
    kv[:, width : width + LANES] = jnp.where(lane == row_seg, -BIG, 0.0).astype(jnp.bfloat16)
    kv[:, width + LANES :] = v_ref[...]
    other = jnp.where(lane == row_seg, 0.0, jnp.where(lane < 4, 1.0, 0.0)).astype(jnp.bfloat16)
    for tile in range(2):
        part = other[tile * TILE : (tile + 1) * TILE]
        query_seg[2 * tile * TILE : (2 * tile + 1) * TILE, :] = part
        query_seg[(2 * tile + 1) * TILE : (2 * tile + 2) * TILE, :] = part

    pl.semaphore_wait(barrier, len(masks) + 2)

    def halo_copy(way):
        source = kv.at[TILE : 2 * TILE] if way == 0 else kv.at[0:TILE]
        return pltpu.make_async_remote_copy(
            src_ref=source, dst_ref=left if way == 0 else right,
            send_sem=halo_send.at[way], recv_sem=halo_recv.at[way],
            device_id={"seq": after if way == 0 else before},
            device_id_type=pl.DeviceIdType.MESH)

    has_right = me < devices - 1
    has_left = me > 0

    @pl.when(has_right)
    def _():
        halo_copy(0).start()

    @pl.when(has_left)
    def _():
        halo_copy(1).start()

    def edge(ref):
        ref[...] = jnp.zeros(ref.shape, ref.dtype)
        spot = lax.broadcasted_iota(jnp.int32, (TILE, LANES), 1)
        ref[:, width : width + LANES] = jnp.where(spot == 3, -BIG, 0.0).astype(jnp.bfloat16)

    @pl.when(me == 0)
    def _():
        edge(left)

    @pl.when(me == devices - 1)
    def _():
        edge(right)

    slots = []
    count = 0
    for _, _, some, _ in plans:
        slots.append(count)
        count += len(some)

    def level_copy(index, c):
        rows, shared, some, _ = plans[index]
        spot = (me % (1 << index)) // (1 << shared) * rows
        return pltpu.make_async_remote_copy(
            src_ref=pieces[index],
            dst_ref=blocks[index].at[pl.ds(pl.multiple_of(spot, MIN_ROWS), rows)],
            send_sem=send.at[slots[index] + c], recv_sem=recv.at[slots[index] + c],
            device_id=to(some[c]), device_id_type=pl.DeviceIdType.MESH)

    def forward_copy(index, c):
        rows, _, some, _ = plans[index]
        spot = pl.multiple_of((flip(me, some[c]) % (1 << index)) * rows, MIN_ROWS)
        part = blocks[index].at[pl.ds(spot, rows)]
        return pltpu.make_async_remote_copy(
            src_ref=part, dst_ref=part,
            send_sem=fsend.at[slots[index] + c], recv_sem=frecv.at[slots[index] + c],
            device_id=to(1), device_id_type=pl.DeviceIdType.MESH)

    for index in range(levels):
        if index == 0:
            pieces[0][...] = halve(kv[...])
        elif index < 4:
            pieces[index][...] = halve(pieces[index - 1][...])
        else:
            join = joins[index - 4]
            mask = 1 << (index - 4)
            half = pl.ds(pl.multiple_of((me // mask) % 2 * MIN_ROWS, MIN_ROWS), MIN_ROWS)
            join[half, :] = pieces[index - 1][...]
            copy = pltpu.make_async_remote_copy(
                src_ref=pieces[index - 1], dst_ref=join.at[half],
                send_sem=jsend.at[index - 4], recv_sem=jrecv.at[index - 4],
                device_id=to(mask), device_id_type=pl.DeviceIdType.MESH)
            copy.start()
            copy.wait()
            pieces[index][...] = halve(join[...])
        for c in range(len(plans[index][2])):
            level_copy(index, c).start()

    ones = jnp.ones((TILE, LANES), jnp.bfloat16)

    def weigh(scores, top, values, keys):
        weights = jnp.exp(scores - top).astype(jnp.bfloat16)
        right_side = jnp.concatenate([values, jnp.ones((keys, LANES), jnp.bfloat16)], axis=1)
        return jnp.dot(weights, right_side, preferred_element_type=jnp.float32)

    def score(left_side, key_part, seg_part):
        right_side = jnp.concatenate([key_part, seg_part], axis=1)
        return lax.dot_general(left_side, right_side, (((1,), (1,)), ((), ())),
                               preferred_element_type=jnp.float32)

    def columns(pair):
        return (pl.ds(pl.multiple_of(pair * LANES, LANES), LANES),
                pl.ds(pl.multiple_of(width + LANES + pair * LANES, LANES), LANES))

    seg_columns = slice(width, width + LANES)

    @pl.loop(0, pairs)
    def _(pair):
        key_cols, value_cols = columns(pair)
        scaled = q_ref[:, key_cols] * jnp.bfloat16(DH**-0.5)
        spot = lax.broadcasted_iota(jnp.int32, (tokens, LANES), 1)
        zero = jnp.zeros_like(scaled)
        low = jnp.where(spot < DH, scaled, zero)
        high = jnp.where(spot < DH, zero, scaled)
        both = jnp.concatenate([low[:TILE], high[:TILE], low[TILE:], high[TILE:]], axis=0)
        queries[pair] = both
        scores = score(jnp.concatenate([both, query_seg[...]], axis=1), kv[:, key_cols],
                       kv[:, seg_columns])
        top = jnp.max(scores, axis=1, keepdims=True)
        largest[pair] = jnp.broadcast_to(top, (2 * tokens, LANES))
        total[pair] = weigh(scores, top, kv[:, value_cols], tokens)

    def far_phase(indices):
        @pl.loop(0, pairs)
        def _(pair):
            key_cols, value_cols = columns(pair)
            left_side = jnp.concatenate([queries[pair], query_seg[...]], axis=1)
            scores = [score(left_side, blocks[i][:, key_cols], blocks[i][:, seg_columns])
                      for i in indices]
            old = largest[pair][:, :1]
            top = old
            for some in scores:
                top = jnp.maximum(top, jnp.max(some, axis=1, keepdims=True))
            acc = total[pair] * jnp.exp(old - top)
            for i, some in zip(indices, scores):
                acc = acc + weigh(some, top, blocks[i][:, value_cols], TILE)
            total[pair] = acc
            largest[pair] = jnp.broadcast_to(top, (2 * tokens, LANES))

    level_copy(0, 0).wait_recv()
    far_phase([0])

    for index in range(1, levels):
        for c in range(len(plans[index][2])):
            level_copy(index, c).wait_recv()
            if plans[index][3]:
                forward_copy(index, c).start()

    @pl.when(has_left)
    def _():
        halo_copy(0).wait_recv()

    @pl.when(has_right)
    def _():
        halo_copy(1).wait_recv()

    @pl.loop(0, pairs)
    def _(pair):
        key_cols, value_cols = columns(pair)
        for tile, halo in ((0, left), (1, right)):
            rows = slice(2 * tile * TILE, 2 * (tile + 1) * TILE)
            left_side = jnp.concatenate([queries[pair, rows], query_seg[rows, :]], axis=1)
            scores = score(left_side, halo[:, key_cols], halo[:, seg_columns])
            old = largest[pair, rows][:, :1]
            top = jnp.maximum(old, jnp.max(scores, axis=1, keepdims=True))
            total[pair, rows] = total[pair, rows] * jnp.exp(old - top) + weigh(
                scores, top, halo[:, value_cols], TILE)
            largest[pair, rows] = jnp.broadcast_to(top, (2 * TILE, LANES))

    for index in range(1, levels):
        if plans[index][3]:
            for c in range(len(plans[index][2])):
                forward_copy(index, c).wait_recv()
    rest_levels = list(range(1, levels))
    while rest_levels:
        far_phase(rest_levels[:3])
        rest_levels = rest_levels[3:]

    @pl.loop(0, pairs)
    def _(pair):
        key_cols, _ = columns(pair)
        spot = lax.broadcasted_iota(jnp.int32, (TILE, LANES), 1)
        for tile in range(2):
            base = 2 * tile * TILE
            one = total[pair, base : base + TILE]
            two = total[pair, base + TILE : base + 2 * TILE]
            top = jnp.where(spot < DH, one[:, :LANES], two[:, :LANES])
            bottom = jnp.where(spot < DH, one[:, LANES:], two[:, LANES:])
            context[tile * TILE : (tile + 1) * TILE, key_cols] = (top / bottom).astype(jnp.bfloat16)

    w_copy.wait()

    @pl.loop(0, out_ref.shape[1] // 256)
    def _(part):
        cols = pl.ds(pl.multiple_of(part * 256, 256), 256)
        out_ref[:, cols] = jnp.dot(context[...], w_vmem[:, cols],
                                   preferred_element_type=jnp.float32).astype(jnp.bfloat16)

    for index in range(levels):
        for c in range(len(plans[index][2])):
            level_copy(index, c).wait_send()
            if plans[index][3]:
                forward_copy(index, c).wait_send()

    @pl.when(has_right)
    def _():
        halo_copy(0).wait_send()

    @pl.when(has_left)
    def _():
        halo_copy(1).wait_send()


def on_device(devices, query_rows, key_rows, value_rows, segment_ids, out_weight):
    tokens, width = query_rows.shape
    levels = devices.bit_length() - 1
    span = 2 * width + LANES
    plans = [level_plan(level) for level in range(1, levels + 1)]
    copies = sum(len(plan[2]) for plan in plans)
    pairs = width // LANES
    bf16 = jnp.bfloat16
    scratch = [
        pltpu.VMEM((tokens, span), bf16),
        pltpu.VMEM((TILE, span), bf16),
        pltpu.VMEM((TILE, span), bf16),
        pltpu.VMEM((pairs, 2 * tokens, LANES), bf16),
        pltpu.VMEM((2 * tokens, LANES), bf16),
        pltpu.VMEM((pairs, 2 * tokens, LANES), jnp.float32),
        pltpu.VMEM((pairs, 2 * tokens, 2 * LANES), jnp.float32),
        pltpu.VMEM((tokens, width), bf16),
        pltpu.VMEM(out_weight.shape, bf16),
        pltpu.SemaphoreType.DMA,
        pltpu.SemaphoreType.DMA((2,)),
        pltpu.SemaphoreType.DMA((2,)),
    ]
    scratch += [pltpu.VMEM((plan[0], span), bf16) for plan in plans]
    scratch += [pltpu.VMEM((TILE, span), bf16) for _ in plans]
    scratch += [pltpu.SemaphoreType.DMA((copies,)) for _ in range(4)]
    if levels > 4:
        scratch += [pltpu.VMEM((2 * MIN_ROWS, span), bf16) for _ in range(levels - 4)]
        scratch += [pltpu.SemaphoreType.DMA((levels - 4,)) for _ in range(2)]
    vmem = pl.BlockSpec(memory_space=pltpu.VMEM)
    return pl.pallas_call(
        functools.partial(attend, devices),
        out_shape=jax.ShapeDtypeStruct((tokens, width), bf16),
        in_specs=[vmem, vmem, vmem, vmem, pl.BlockSpec(memory_space=pl.ANY)],
        out_specs=vmem,
        scratch_shapes=scratch,
        compiler_params=pltpu.CompilerParams(
            collective_id=0, has_side_effects=True, vmem_limit_bytes=48 * 1024 * 1024),
    )(query_rows, key_rows, value_rows, segment_ids.reshape(1, tokens), out_weight)


def solution(mesh):
    rows = P(("groups", "seq"), None)
    return jax.shard_map(
        functools.partial(on_device, mesh.shape["seq"]), mesh=mesh,
        in_specs=(rows, rows, rows, P(("groups", "seq")), P()),
        out_specs=rows, check_vma=False)
```

profile of v0, /device:TPU:5, one launch (start us, length us, event | category | flops | bytes accessed | tf_op | source)
XLA Modules:
  0.0 56.0 jit_solution(1901954949581436172)
XLA Ops:
  0.0 0.0 copy-start
  0.0 1.6 %copy-done = bf16[1024,1024]{1,0:T(8,128)(2,1)S(1)} copy-done((bf16[1024,1024]{1,0:T(8,128)(2,1)S(1)}, bf16[1024,1024]{1,0:T(8,128)(2,1)}, u32[]{:S(2)}) %copy-start) | copy-done | bytes 2097176
  1.6 0.0 copy-start.1
  1.6 1.0 %copy-done.1 = bf16[256,1024]{1,0:T(8,128)(2,1)S(1)} copy-done((bf16[256,1024]{1,0:T(8,128)(2,1)S(1)}, bf16[256,1024]{1,0:T(8,128)(2,1)}, u32[]{:S(2)}) %copy-start.1) | copy-done | bytes 524312
  2.6 0.0 copy-start.2
  2.6 1.0 %copy-done.2 = bf16[256,1024]{1,0:T(8,128)(2,1)S(1)} copy-done((bf16[256,1024]{1,0:T(8,128)(2,1)S(1)}, bf16[256,1024]{1,0:T(8,128)(2,1)}, u32[]{:S(2)}) %copy-start.2) | copy-done | bytes 524312
  3.7 0.0 copy-start.3
  3.7 1.0 %copy-done.3 = bf16[256,1024]{1,0:T(8,128)(2,1)S(1)} copy-done((bf16[256,1024]{1,0:T(8,128)(2,1)S(1)}, bf16[256,1024]{1,0:T(8,128)(2,1)}, u32[]{:S(2)}) %copy-start.3) | copy-done | bytes 524312
  4.7 0.0 copy-start.4
  4.7 0.7 %copy-done.4 = s32[256]{0:T(256)S(1)} copy-done((s32[256]{0:T(256)S(1)}, s32[256]{0:T(256)}, u32[]{:S(2)}) %copy-start.4) | copy-done | bytes 1048
  5.4 49.8 %shard_map.55 = bf16[256,1024]{1,0:T(8,128)(2,1)S(1)} custom-call(bf16[256,1024]{1,0:T(8,128)(2,1)S(1)} %copy-done.1, bf16[256,1024]{1,0:T(8,128)(2,1)S(1)} %copy-done.2, bf16[256,1024]{1,0:T(8,128)(2,1)S(1)} %copy-done.3, s32[1,256]{1,0:T(1,128)S(1)} %bitcast.1, bf16[1024,1024]{1,0:T(8,128)(2,1)S(1)} %copy-done), custom_call_target="tpu_custom_call" | custom-call | tf_op jit(solution)/shard_map/pallas_call | solution.py:326
  55.2 0.8 %copy.7 = bf16[256,1024]{1,0:T(8,128)(2,1)} copy(bf16[256,1024]{1,0:T(8,128)(2,1)S(1)} %shard_map.55) | data formatting | bytes 1048576
Async XLA Ops:
  0.0 1.6 %copy-start = (bf16[1024,1024]{1,0:T(8,128)(2,1)S(1)}, bf16[1024,1024]{1,0:T(8,128)(2,1)}, u32[]{:S(2)}) copy-start(bf16[1024,1024]{1,0:T(8,128)(2,1)} %w_hbm.1) | copy-start | bytes 6291460
  1.6 1.0 %copy-start.1 = (bf16[256,1024]{1,0:T(8,128)(2,1)S(1)}, bf16[256,1024]{1,0:T(8,128)(2,1)}, u32[]{:S(2)}) copy-start(bf16[256,1024]{1,0:T(8,128)(2,1)} %q_ref.1) | copy-start | bytes 1572868
  2.6 1.0 %copy-start.2 = (bf16[256,1024]{1,0:T(8,128)(2,1)S(1)}, bf16[256,1024]{1,0:T(8,128)(2,1)}, u32[]{:S(2)}) copy-start(bf16[256,1024]{1,0:T(8,128)(2,1)} %k_ref.1) | copy-start | bytes 1572868
  3.7 1.0 %copy-start.3 = (bf16[256,1024]{1,0:T(8,128)(2,1)S(1)}, bf16[256,1024]{1,0:T(8,128)(2,1)}, u32[]{:S(2)}) copy-start(bf16[256,1024]{1,0:T(8,128)(2,1)} %v_ref.1) | copy-start | bytes 1572868
  4.7 0.7 %copy-start.4 = (s32[256]{0:T(256)S(1)}, s32[256]{0:T(256)}, u32[]{:S(2)}) copy-start(s32[256]{0:T(256)} %param.8) | copy-start | bytes 3076
where the time goes:
time: 56.3 us; the launch traced here: 56 us
  Pallas kernels  49.8 us (88%)
  local copies, waits for them, and re-layouts  6.19 us (11%)
    pallas_call x1, Pallas kernels, on_device(): pl.pallas_call(functools.partial(attend, devices), out_shape=jax.ShapeDty...  49.8 us
    unnamed x11, local copies, waits for them, and re-layouts  6.19 us

commit v1 on v0

--- a/solution.py
+++ b/solution.py
@@ -86,10 +86,8 @@
     kv[:, width : width + LANES] = jnp.where(lane == row_seg, -BIG, 0.0).astype(jnp.bfloat16)
     kv[:, width + LANES :] = v_ref[...]
     other = jnp.where(lane == row_seg, 0.0, jnp.where(lane < 4, 1.0, 0.0)).astype(jnp.bfloat16)
-    for tile in range(2):
-        part = other[tile * TILE : (tile + 1) * TILE]
-        query_seg[2 * tile * TILE : (2 * tile + 1) * TILE, :] = part
-        query_seg[(2 * tile + 1) * TILE : (2 * tile + 2) * TILE, :] = part
+    query_seg[:tokens, :] = other
+    query_seg[tokens:, :] = other
 
     pl.semaphore_wait(barrier, len(masks) + 2)
 
@@ -103,14 +101,6 @@
 
     has_right = me < devices - 1
     has_left = me > 0
-
-    @pl.when(has_right)
-    def _():
-        halo_copy(0).start()
-
-    @pl.when(has_left)
-    def _():
-        halo_copy(1).start()
 
     def edge(ref):
         ref[...] = jnp.zeros(ref.shape, ref.dtype)
@@ -169,107 +159,122 @@
         for c in range(len(plans[index][2])):
             level_copy(index, c).start()
 
-    ones = jnp.ones((TILE, LANES), jnp.bfloat16)
-
-    def weigh(scores, top, values, keys):
-        weights = jnp.exp(scores - top).astype(jnp.bfloat16)
-        right_side = jnp.concatenate([values, jnp.ones((keys, LANES), jnp.bfloat16)], axis=1)
-        return jnp.dot(weights, right_side, preferred_element_type=jnp.float32)
-
-    def score(left_side, key_part, seg_part):
-        right_side = jnp.concatenate([key_part, seg_part], axis=1)
-        return lax.dot_general(left_side, right_side, (((1,), (1,)), ((), ())),
-                               preferred_element_type=jnp.float32)
+    @pl.when(has_right)
+    def _():
+        halo_copy(0).start()
+
+    @pl.when(has_left)
+    def _():
+        halo_copy(1).start()
+
+    spot = lax.broadcasted_iota(jnp.int32, (TILE, LANES), 1)
+    low_lanes = spot < DH
+    one = jnp.ones((TILE, LANES), jnp.bfloat16)
+    zero = jnp.zeros((TILE, LANES), jnp.bfloat16)
+    low_ones = jnp.where(low_lanes, one, zero)
+    high_ones = jnp.where(low_lanes, zero, one)
+    seg_columns = slice(width, width + LANES)
 
     def columns(pair):
         return (pl.ds(pl.multiple_of(pair * LANES, LANES), LANES),
                 pl.ds(pl.multiple_of(width + LANES + pair * LANES, LANES), LANES))
 
-    seg_columns = slice(width, width + LANES)
+    def score(left_side, ref, base, pair):
+        key_cols, _ = columns(pair)
+        rows = slice(base, base + TILE)
+        right_side = jnp.concatenate([ref[rows, key_cols], ref[rows, seg_columns]], axis=1)
+        return lax.dot_general(left_side, right_side, (((1,), (1,)), ((), ())),
+                               preferred_element_type=jnp.float32)
+
+    def highest(scores):
+        top = scores[0]
+        for some in scores[1:]:
+            top = jnp.maximum(top, some)
+        return jnp.broadcast_to(jnp.max(top, axis=1, keepdims=True), top.shape)
+
+    def weigh(scores, top, spots, pair):
+        _, value_cols = columns(pair)
+        half = top.shape[0] // 2
+        left_side, right_side = [], []
+        for some, (ref, base) in zip(scores, spots):
+            weights = jnp.exp(some - top).astype(jnp.bfloat16)
+            values = ref[slice(base, base + TILE), value_cols]
+            left_side += [weights[:half], weights[half:]]
+            right_side += [
+                jnp.concatenate([jnp.where(low_lanes, values, zero), low_ones], axis=1),
+                jnp.concatenate([jnp.where(low_lanes, zero, values), high_ones], axis=1),
+            ]
+        return jnp.dot(jnp.concatenate(left_side, axis=1), jnp.concatenate(right_side, axis=0),
+                       preferred_element_type=jnp.float32)
+
+    def rescale(old, top):
+        shrink = jnp.exp(old - top)
+        half = top.shape[0] // 2
+        lanes = lax.broadcasted_iota(jnp.int32, (half, LANES), 1) < DH
+        both = jnp.where(lanes, shrink[:half], shrink[half:])
+        return jnp.concatenate([both, both], axis=1)
+
+    near = [(kv, 0), (kv, TILE)]
+
+    level_copy(0, 0).wait_recv()
 
     @pl.loop(0, pairs)
     def _(pair):
-        key_cols, value_cols = columns(pair)
+        key_cols, _ = columns(pair)
         scaled = q_ref[:, key_cols] * jnp.bfloat16(DH**-0.5)
-        spot = lax.broadcasted_iota(jnp.int32, (tokens, LANES), 1)
-        zero = jnp.zeros_like(scaled)
-        low = jnp.where(spot < DH, scaled, zero)
-        high = jnp.where(spot < DH, zero, scaled)
-        both = jnp.concatenate([low[:TILE], high[:TILE], low[TILE:], high[TILE:]], axis=0)
+        lanes = lax.broadcasted_iota(jnp.int32, (tokens, LANES), 1) < DH
+        none = jnp.zeros_like(scaled)
+        both = jnp.concatenate([jnp.where(lanes, scaled, none), jnp.where(lanes, none, scaled)],
+                               axis=0)
         queries[pair] = both
-        scores = score(jnp.concatenate([both, query_seg[...]], axis=1), kv[:, key_cols],
-                       kv[:, seg_columns])
-        top = jnp.max(scores, axis=1, keepdims=True)
-        largest[pair] = jnp.broadcast_to(top, (2 * tokens, LANES))
-        total[pair] = weigh(scores, top, kv[:, value_cols], tokens)
-
-    def far_phase(indices):
-        @pl.loop(0, pairs)
-        def _(pair):
-            key_cols, value_cols = columns(pair)
-            left_side = jnp.concatenate([queries[pair], query_seg[...]], axis=1)
-            scores = [score(left_side, blocks[i][:, key_cols], blocks[i][:, seg_columns])
-                      for i in indices]
-            old = largest[pair][:, :1]
-            top = old
-            for some in scores:
-                top = jnp.maximum(top, jnp.max(some, axis=1, keepdims=True))
-            acc = total[pair] * jnp.exp(old - top)
-            for i, some in zip(indices, scores):
-                acc = acc + weigh(some, top, blocks[i][:, value_cols], TILE)
-            total[pair] = acc
-            largest[pair] = jnp.broadcast_to(top, (2 * tokens, LANES))
-
-    level_copy(0, 0).wait_recv()
-    far_phase([0])
+        spots = near + [(blocks[0], 0)]
+        left_side = jnp.concatenate([both, query_seg[...]], axis=1)
+        scores = [score(left_side, ref, base, pair) for ref, base in spots]
+        top = highest(scores)
+        largest[pair] = top
+        total[pair] = weigh(scores, top, spots, pair)
 
     for index in range(1, levels):
         for c in range(len(plans[index][2])):
             level_copy(index, c).wait_recv()
             if plans[index][3]:
                 forward_copy(index, c).start()
-
-    @pl.when(has_left)
-    def _():
-        halo_copy(0).wait_recv()
-
-    @pl.when(has_right)
-    def _():
-        halo_copy(1).wait_recv()
-
-    @pl.loop(0, pairs)
-    def _(pair):
-        key_cols, value_cols = columns(pair)
-        for tile, halo in ((0, left), (1, right)):
-            rows = slice(2 * tile * TILE, 2 * (tile + 1) * TILE)
-            left_side = jnp.concatenate([queries[pair, rows], query_seg[rows, :]], axis=1)
-            scores = score(left_side, halo[:, key_cols], halo[:, seg_columns])
-            old = largest[pair, rows][:, :1]
-            top = jnp.maximum(old, jnp.max(scores, axis=1, keepdims=True))
-            total[pair, rows] = total[pair, rows] * jnp.exp(old - top) + weigh(
-                scores, top, halo[:, value_cols], TILE)
-            largest[pair, rows] = jnp.broadcast_to(top, (2 * TILE, LANES))
-
     for index in range(1, levels):
         if plans[index][3]:
             for c in range(len(plans[index][2])):
                 forward_copy(index, c).wait_recv()
-    rest_levels = list(range(1, levels))
-    while rest_levels:
-        far_phase(rest_levels[:3])
-        rest_levels = rest_levels[3:]
+
+    @pl.loop(0, pairs)
+    def _(pair):
+        left_side = jnp.concatenate([queries[pair], query_seg[...]], axis=1)
+        spots = [(blocks[index], 0) for index in range(1, levels)]
+        scores = [score(left_side, ref, base, pair) for ref, base in spots]
+        old = largest[pair]
+        top = jnp.maximum(old, highest(scores))
+        largest[pair] = top
+        total[pair] = total[pair] * rescale(old, top) + weigh(scores, top, spots, pair)
+
+    @pl.when(has_left)
+    def _():
+        halo_copy(0).wait_recv()
+
+    @pl.when(has_right)
+    def _():
+        halo_copy(1).wait_recv()
 
     @pl.loop(0, pairs)
     def _(pair):
         key_cols, _ = columns(pair)
-        spot = lax.broadcasted_iota(jnp.int32, (TILE, LANES), 1)
-        for tile in range(2):
-            base = 2 * tile * TILE
-            one = total[pair, base : base + TILE]
-            two = total[pair, base + TILE : base + 2 * TILE]
-            top = jnp.where(spot < DH, one[:, :LANES], two[:, :LANES])
-            bottom = jnp.where(spot < DH, one[:, LANES:], two[:, LANES:])
-            context[tile * TILE : (tile + 1) * TILE, key_cols] = (top / bottom).astype(jnp.bfloat16)
+        for tile, halo in ((0, left), (1, right)):
+            one_head = slice(tile * TILE, (tile + 1) * TILE)
+            two_head = slice(tokens + tile * TILE, tokens + (tile + 1) * TILE)
+            part = jnp.concatenate([queries[pair, one_head], queries[pair, two_head]], axis=0)
+            seg_part = jnp.concatenate([query_seg[one_head, :], query_seg[two_head, :]], axis=0)
+            scores = [score(jnp.concatenate([part, seg_part], axis=1), halo, 0, pair)]
+            old = jnp.concatenate([largest[pair, one_head], largest[pair, two_head]], axis=0)
+            top = jnp.maximum(old, highest(scores))
+            acc = total[pair, one_head] * rescale(old, top) + weigh(scores, top, [(halo, 0)], pair)
+            context[one_head, key_cols] = (acc[:, :LANES] / acc[:, LANES:]).astype(jnp.bfloat16)
 
     w_copy.wait()
 
@@ -309,7 +314,7 @@
         pltpu.VMEM((pairs, 2 * tokens, LANES), bf16),
         pltpu.VMEM((2 * tokens, LANES), bf16),
         pltpu.VMEM((pairs, 2 * tokens, LANES), jnp.float32),
-        pltpu.VMEM((pairs, 2 * tokens, 2 * LANES), jnp.float32),
+        pltpu.VMEM((pairs, tokens, 2 * LANES), jnp.float32),
         pltpu.VMEM((tokens, width), bf16),
         pltpu.VMEM(out_weight.shape, bf16),
         pltpu.SemaphoreType.DMA,

time: 56.3 us -> 48.5 us (0.86)
  Pallas kernels: 49.8 us -> 42 us
    pallas_call x1, Pallas kernels: 49.8 us -> 42 us  [on_device(): pl.pallas_call(functools.partial(attend, devices), out_shape=jax.ShapeDty...]
where the time goes in v1:
time: 48.5 us; the launch traced here: 48.2 us
  Pallas kernels  42 us (87%)
  local copies, waits for them, and re-layouts  6.19 us (13%)
    pallas_call x1, Pallas kernels, on_device(): pl.pallas_call(functools.partial(attend, devices), out_shape=jax.ShapeDty...  42 us
    unnamed x11, local copies, waits for them, and re-layouts  6.19 us

profile of v1, /device:TPU:5, one launch (start us, length us, event | category | flops | bytes accessed | tf_op | source)
XLA Modules:
  0.0 48.2 jit_solution(13749479771082660262)
XLA Ops:
  0.0 0.0 copy-start
  0.0 1.6 %copy-done = bf16[1024,1024]{1,0:T(8,128)(2,1)S(1)} copy-done((bf16[1024,1024]{1,0:T(8,128)(2,1)S(1)}, bf16[1024,1024]{1,0:T(8,128)(2,1)}, u32[]{:S(2)}) %copy-start) | copy-done | bytes 2097176
  1.6 0.0 copy-start.1
  1.6 1.0 %copy-done.1 = bf16[256,1024]{1,0:T(8,128)(2,1)S(1)} copy-done((bf16[256,1024]{1,0:T(8,128)(2,1)S(1)}, bf16[256,1024]{1,0:T(8,128)(2,1)}, u32[]{:S(2)}) %copy-start.1) | copy-done | bytes 524312
  2.6 0.0 copy-start.2
  2.6 1.0 %copy-done.2 = bf16[256,1024]{1,0:T(8,128)(2,1)S(1)} copy-done((bf16[256,1024]{1,0:T(8,128)(2,1)S(1)}, bf16[256,1024]{1,0:T(8,128)(2,1)}, u32[]{:S(2)}) %copy-start.2) | copy-done | bytes 524312
  3.7 0.0 copy-start.3
  3.7 1.0 %copy-done.3 = bf16[256,1024]{1,0:T(8,128)(2,1)S(1)} copy-done((bf16[256,1024]{1,0:T(8,128)(2,1)S(1)}, bf16[256,1024]{1,0:T(8,128)(2,1)}, u32[]{:S(2)}) %copy-start.3) | copy-done | bytes 524312
  4.7 0.0 copy-start.4
  4.7 0.7 %copy-done.4 = s32[256]{0:T(256)S(1)} copy-done((s32[256]{0:T(256)S(1)}, s32[256]{0:T(256)}, u32[]{:S(2)}) %copy-start.4) | copy-done | bytes 1048
  5.4 42.0 %shard_map.55 = bf16[256,1024]{1,0:T(8,128)(2,1)S(1)} custom-call(bf16[256,1024]{1,0:T(8,128)(2,1)S(1)} %copy-done.1, bf16[256,1024]{1,0:T(8,128)(2,1)S(1)} %copy-done.2, bf16[256,1024]{1,0:T(8,128)(2,1)S(1)} %copy-done.3, s32[1,256]{1,0:T(1,128)S(1)} %bitcast.1, bf16[1024,1024]{1,0:T(8,128)(2,1)S(1)} %copy-done), custom_call_target="tpu_custom_call" | custom-call | tf_op jit(solution)/shard_map/pallas_call | solution.py:331
  47.4 0.8 %copy.7 = bf16[256,1024]{1,0:T(8,128)(2,1)} copy(bf16[256,1024]{1,0:T(8,128)(2,1)S(1)} %shard_map.55) | data formatting | bytes 1048576
Async XLA Ops:
  0.0 1.6 %copy-start = (bf16[1024,1024]{1,0:T(8,128)(2,1)S(1)}, bf16[1024,1024]{1,0:T(8,128)(2,1)}, u32[]{:S(2)}) copy-start(bf16[1024,1024]{1,0:T(8,128)(2,1)} %w_hbm.1) | copy-start | bytes 6291460
  1.6 1.0 %copy-start.1 = (bf16[256,1024]{1,0:T(8,128)(2,1)S(1)}, bf16[256,1024]{1,0:T(8,128)(2,1)}, u32[]{:S(2)}) copy-start(bf16[256,1024]{1,0:T(8,128)(2,1)} %q_ref.1) | copy-start | bytes 1572868
  2.6 1.0 %copy-start.2 = (bf16[256,1024]{1,0:T(8,128)(2,1)S(1)}, bf16[256,1024]{1,0:T(8,128)(2,1)}, u32[]{:S(2)}) copy-start(bf16[256,1024]{1,0:T(8,128)(2,1)} %k_ref.1) | copy-start | bytes 1572868
  3.7 1.0 %copy-start.3 = (bf16[256,1024]{1,0:T(8,128)(2,1)S(1)}, bf16[256,1024]{1,0:T(8,128)(2,1)}, u32[]{:S(2)}) copy-start(bf16[256,1024]{1,0:T(8,128)(2,1)} %v_ref.1) | copy-start | bytes 1572868
  4.7 0.7 %copy-start.4 = (s32[256]{0:T(256)S(1)}, s32[256]{0:T(256)}, u32[]{:S(2)}) copy-start(s32[256]{0:T(256)} %param.8) | copy-start | bytes 3076

commit v2 on v1

--- a/solution.py
+++ b/solution.py
@@ -39,7 +39,7 @@
     return jnp.dot(pick, source, preferred_element_type=jnp.float32).astype(jnp.bfloat16)
 
 
-def attend(devices, q_ref, k_ref, v_ref, seg_ref, w_hbm, out_ref, kv, left, right, queries,
+def attend(devices, q_hbm, k_hbm, v_hbm, seg_hbm, w_hbm, out_ref, q_ref, seg_ref, load_sem, kv, left, right, queries,
            query_seg, largest, total, context, w_vmem, w_sem, halo_send, halo_recv, *rest):
     levels = devices.bit_length() - 1
     pieces = rest[:levels]
@@ -49,7 +49,7 @@
     if levels > 4:
         jsend, jrecv = rest[-2:]
     me = lax.axis_index("seq")
-    width = q_ref.shape[1]
+    width = q_hbm.shape[1]
     pairs = width // LANES
     plans = [level_plan(level) for level in range(1, levels + 1)]
 
@@ -72,23 +72,32 @@
         pl.semaphore_signal(barrier, inc=1, device_id={"seq": target},
                             device_id_type=pl.DeviceIdType.MESH)
 
+    loads = [
+        pltpu.make_async_copy(seg_hbm, seg_ref, load_sem.at[0]),
+        pltpu.make_async_copy(k_hbm, kv.at[:, 0:width], load_sem.at[1]),
+        pltpu.make_async_copy(v_hbm, kv.at[:, width + LANES : 2 * width + LANES], load_sem.at[2]),
+        pltpu.make_async_copy(q_hbm, q_ref, load_sem.at[3]),
+    ]
+    for load in loads:
+        load.start()
     w_copy = pltpu.make_async_copy(w_hbm, w_vmem, w_sem)
     w_copy.start()
-
-    tokens = q_ref.shape[0]
+    loads[0].wait()
+
+    tokens = q_hbm.shape[0]
     seg = seg_ref[...]
     first = jnp.sum(jnp.where(seg < 1, 1.0, 0.0), axis=1, keepdims=True)
     second = jnp.sum(jnp.where(seg < 2, 1.0, 0.0), axis=1, keepdims=True)
     row = lax.broadcasted_iota(jnp.int32, (tokens, LANES), 0).astype(jnp.float32)
     lane = lax.broadcasted_iota(jnp.int32, (tokens, LANES), 1).astype(jnp.float32)
     row_seg = jnp.where(row >= first, 1.0, 0.0) + jnp.where(row >= second, 1.0, 0.0)
-    kv[:, :width] = k_ref[...]
     kv[:, width : width + LANES] = jnp.where(lane == row_seg, -BIG, 0.0).astype(jnp.bfloat16)
-    kv[:, width + LANES :] = v_ref[...]
     other = jnp.where(lane == row_seg, 0.0, jnp.where(lane < 4, 1.0, 0.0)).astype(jnp.bfloat16)
     query_seg[:tokens, :] = other
     query_seg[tokens:, :] = other
 
+    loads[1].wait()
+    loads[2].wait()
     pl.semaphore_wait(barrier, len(masks) + 2)
 
     def halo_copy(way):
@@ -159,14 +168,6 @@
         for c in range(len(plans[index][2])):
             level_copy(index, c).start()
 
-    @pl.when(has_right)
-    def _():
-        halo_copy(0).start()
-
-    @pl.when(has_left)
-    def _():
-        halo_copy(1).start()
-
     spot = lax.broadcasted_iota(jnp.int32, (TILE, LANES), 1)
     low_lanes = spot < DH
     one = jnp.ones((TILE, LANES), jnp.bfloat16)
@@ -215,6 +216,7 @@
         return jnp.concatenate([both, both], axis=1)
 
     near = [(kv, 0), (kv, TILE)]
+    loads[3].wait()
 
     level_copy(0, 0).wait_recv()
 
@@ -239,6 +241,14 @@
             level_copy(index, c).wait_recv()
             if plans[index][3]:
                 forward_copy(index, c).start()
+    @pl.when(has_right)
+    def _():
+        halo_copy(0).start()
+
+    @pl.when(has_left)
+    def _():
+        halo_copy(1).start()
+
     for index in range(1, levels):
         if plans[index][3]:
             for c in range(len(plans[index][2])):
@@ -308,6 +318,9 @@
     pairs = width // LANES
     bf16 = jnp.bfloat16
     scratch = [
+        pltpu.VMEM((tokens, width), bf16),
+        pltpu.VMEM((1, tokens), jnp.int32),
+        pltpu.SemaphoreType.DMA((4,)),
         pltpu.VMEM((tokens, span), bf16),
         pltpu.VMEM((TILE, span), bf16),
         pltpu.VMEM((TILE, span), bf16),
@@ -331,11 +344,11 @@
     return pl.pallas_call(
         functools.partial(attend, devices),
         out_shape=jax.ShapeDtypeStruct((tokens, width), bf16),
-        in_specs=[vmem, vmem, vmem, vmem, pl.BlockSpec(memory_space=pl.ANY)],
+        in_specs=[pl.BlockSpec(memory_space=pltpu.HBM)] * 5,
         out_specs=vmem,
         scratch_shapes=scratch,
         compiler_params=pltpu.CompilerParams(
-            collective_id=0, has_side_effects=True, vmem_limit_bytes=48 * 1024 * 1024),
+            collective_id=0, has_side_effects=True),
     )(query_rows, key_rows, value_rows, segment_ids.reshape(1, tokens), out_weight)
 
 

time: 48.5 us -> 42.1 us (0.87)
  the two profiles are of different devices: /device:TPU:5 before, /device:TPU:6 now
where the time goes in v2:
time: 42.1 us; the launch traced here: 41.8 us
  Pallas kernels  39.9 us (95%)
  local copies, waits for them, and re-layouts  1.87 us (4%)
    pallas_call x1, Pallas kernels, on_device(): pl.pallas_call(functools.partial(attend, devices), out_shape=jax.ShapeDty...  39.9 us
    unnamed x1, local copies, waits for them, and re-layouts  1.87 us

profile of v2, /device:TPU:6, one launch (start us, length us, event | category | flops | bytes accessed | tf_op | source)
XLA Modules:
  0.0 41.8 jit_solution(3867950582824434488)
XLA Ops:
  0.0 39.9 %shard_map.55 = bf16[256,1024]{1,0:T(8,128)(2,1)} custom-call(bf16[256,1024]{1,0:T(8,128)(2,1)} %q_hbm.1, bf16[256,1024]{1,0:T(8,128)(2,1)} %k_hbm.1, bf16[256,1024]{1,0:T(8,128)(2,1)} %v_hbm.1, s32[1,256]{1,0:T(1,128)} %bitcast.1, bf16[1024,1024]{1,0:T(8,128)(2,1)} %w_hbm.1), custom_call_target="tpu_custom_call" | custom-call | tf_op jit(solution)/shard_map/pallas_call | solution.py:344
  39.9 1.9 %copy.7 = bf16[256,1024]{1,0:T(8,128)(2,1)} copy(bf16[256,1024]{1,0:T(8,128)(2,1)} %shard_map.55) | data formatting | bytes 1048576

commit v3 on v2

--- a/solution.py
+++ b/solution.py
@@ -220,7 +220,7 @@
 
     level_copy(0, 0).wait_recv()
 
-    @pl.loop(0, pairs)
+    @pl.loop(0, pairs, unroll=2)
     def _(pair):
         key_cols, _ = columns(pair)
         scaled = q_ref[:, key_cols] * jnp.bfloat16(DH**-0.5)
@@ -236,14 +236,14 @@
         largest[pair] = top
         total[pair] = weigh(scores, top, spots, pair)
 
+    @pl.when(has_right)
+    def _():
+        halo_copy(0).start()
     for index in range(1, levels):
         for c in range(len(plans[index][2])):
             level_copy(index, c).wait_recv()
             if plans[index][3]:
                 forward_copy(index, c).start()
-    @pl.when(has_right)
-    def _():
-        halo_copy(0).start()
 
     @pl.when(has_left)
     def _():
@@ -254,7 +254,7 @@
             for c in range(len(plans[index][2])):
                 forward_copy(index, c).wait_recv()
 
-    @pl.loop(0, pairs)
+    @pl.loop(0, pairs, unroll=2)
     def _(pair):
         left_side = jnp.concatenate([queries[pair], query_seg[...]], axis=1)
         spots = [(blocks[index], 0) for index in range(1, levels)]
@@ -272,7 +272,7 @@
     def _():
         halo_copy(1).wait_recv()
 
-    @pl.loop(0, pairs)
+    @pl.loop(0, pairs, unroll=8)
     def _(pair):
         key_cols, _ = columns(pair)
         for tile, halo in ((0, left), (1, right)):

time: 42.1 us -> 39.1 us (0.929)
  Pallas kernels: 39.9 us -> 36.9 us
    pallas_call x1, Pallas kernels: 39.9 us -> 36.9 us  [on_device(): pl.pallas_call(functools.partial(attend, devices), out_shape=jax.ShapeDty...]
where the time goes in v3:
time: 39.1 us; the launch traced here: 38.8 us
  Pallas kernels  36.9 us (94%)
  local copies, waits for them, and re-layouts  1.87 us (5%)
    pallas_call x1, Pallas kernels, on_device(): pl.pallas_call(functools.partial(attend, devices), out_shape=jax.ShapeDty...  36.9 us
    unnamed x1, local copies, waits for them, and re-layouts  1.87 us

profile of v3, /device:TPU:6, one launch (start us, length us, event | category | flops | bytes accessed | tf_op | source)
XLA Modules:
  0.0 38.8 jit_solution(10958107066076294916)
XLA Ops:
  0.0 36.9 %shard_map.55 = bf16[256,1024]{1,0:T(8,128)(2,1)} custom-call(bf16[256,1024]{1,0:T(8,128)(2,1)} %q_hbm.1, bf16[256,1024]{1,0:T(8,128)(2,1)} %k_hbm.1, bf16[256,1024]{1,0:T(8,128)(2,1)} %v_hbm.1, s32[1,256]{1,0:T(1,128)} %bitcast.1, bf16[1024,1024]{1,0:T(8,128)(2,1)} %w_hbm.1), custom_call_target="tpu_custom_call" | custom-call | tf_op jit(solution)/shard_map/pallas_call | solution.py:344
  36.9 1.9 %copy.7 = bf16[256,1024]{1,0:T(8,128)(2,1)} copy(bf16[256,1024]{1,0:T(8,128)(2,1)} %shard_map.55) | data formatting | bytes 1048576

commit v4 on v3

--- a/solution.py
+++ b/solution.py
@@ -220,7 +220,7 @@
 
     level_copy(0, 0).wait_recv()
 
-    @pl.loop(0, pairs, unroll=2)
+    @pl.loop(0, pairs, unroll=4)
     def _(pair):
         key_cols, _ = columns(pair)
         scaled = q_ref[:, key_cols] * jnp.bfloat16(DH**-0.5)
@@ -254,7 +254,7 @@
             for c in range(len(plans[index][2])):
                 forward_copy(index, c).wait_recv()
 
-    @pl.loop(0, pairs, unroll=2)
+    @pl.loop(0, pairs, unroll=4)
     def _(pair):
         left_side = jnp.concatenate([queries[pair], query_seg[...]], axis=1)
         spots = [(blocks[index], 0) for index in range(1, levels)]
@@ -264,31 +264,37 @@
         largest[pair] = top
         total[pair] = total[pair] * rescale(old, top) + weigh(scores, top, spots, pair)
 
+    def near_phase(pair, tile, halo):
+        key_cols, _ = columns(pair)
+        one_head = slice(tile * TILE, (tile + 1) * TILE)
+        two_head = slice(tokens + tile * TILE, tokens + (tile + 1) * TILE)
+        part = jnp.concatenate([queries[pair, one_head], queries[pair, two_head]], axis=0)
+        seg_part = jnp.concatenate([query_seg[one_head, :], query_seg[two_head, :]], axis=0)
+        scores = [score(jnp.concatenate([part, seg_part], axis=1), halo, 0, pair)]
+        old = jnp.concatenate([largest[pair, one_head], largest[pair, two_head]], axis=0)
+        top = jnp.maximum(old, highest(scores))
+        acc = total[pair, one_head] * rescale(old, top) + weigh(scores, top, [(halo, 0)], pair)
+        context[one_head, key_cols] = (acc[:, :LANES] / acc[:, LANES:]).astype(jnp.bfloat16)
+
     @pl.when(has_left)
     def _():
         halo_copy(0).wait_recv()
-
-    @pl.when(has_right)
-    def _():
-        halo_copy(1).wait_recv()
 
     @pl.loop(0, pairs, unroll=8)
     def _(pair):
-        key_cols, _ = columns(pair)
-        for tile, halo in ((0, left), (1, right)):
-            one_head = slice(tile * TILE, (tile + 1) * TILE)
-            two_head = slice(tokens + tile * TILE, tokens + (tile + 1) * TILE)
-            part = jnp.concatenate([queries[pair, one_head], queries[pair, two_head]], axis=0)
-            seg_part = jnp.concatenate([query_seg[one_head, :], query_seg[two_head, :]], axis=0)
-            scores = [score(jnp.concatenate([part, seg_part], axis=1), halo, 0, pair)]
-            old = jnp.concatenate([largest[pair, one_head], largest[pair, two_head]], axis=0)
-            top = jnp.maximum(old, highest(scores))
-            acc = total[pair, one_head] * rescale(old, top) + weigh(scores, top, [(halo, 0)], pair)
-            context[one_head, key_cols] = (acc[:, :LANES] / acc[:, LANES:]).astype(jnp.bfloat16)
+        near_phase(pair, 0, left)
+
+    @pl.when(has_right)
+    def _():
+        halo_copy(1).wait_recv()
+
+    @pl.loop(0, pairs, unroll=8)
+    def _(pair):
+        near_phase(pair, 1, right)
 
     w_copy.wait()
 
-    @pl.loop(0, out_ref.shape[1] // 256)
+    @pl.loop(0, out_ref.shape[1] // 256, unroll=4)
     def _(part):
         cols = pl.ds(pl.multiple_of(part * 256, 256), 256)
         out_ref[:, cols] = jnp.dot(context[...], w_vmem[:, cols],

time: 39.1 us -> 38.5 us (0.985)
  Pallas kernels: 36.9 us -> 36.5 us
    pallas_call x1, Pallas kernels: 36.9 us -> 36.5 us  [on_device(): pl.pallas_call(functools.partial(attend, devices), out_shape=jax.ShapeDty...]
where the time goes in v4:
time: 38.5 us; the launch traced here: 38.4 us
  Pallas kernels  36.5 us (95%)
  local copies, waits for them, and re-layouts  1.87 us (5%)
    pallas_call x1, Pallas kernels, on_device(): pl.pallas_call(functools.partial(attend, devices), out_shape=jax.ShapeDty...  36.5 us
    unnamed x1, local copies, waits for them, and re-layouts  1.87 us

profile of v4, /device:TPU:6, one launch (start us, length us, event | category | flops | bytes accessed | tf_op | source)
XLA Modules:
  0.0 38.4 jit_solution(12409372658031360843)
XLA Ops:
  0.0 36.5 %shard_map.55 = bf16[256,1024]{1,0:T(8,128)(2,1)} custom-call(bf16[256,1024]{1,0:T(8,128)(2,1)} %q_hbm.1, bf16[256,1024]{1,0:T(8,128)(2,1)} %k_hbm.1, bf16[256,1024]{1,0:T(8,128)(2,1)} %v_hbm.1, s32[1,256]{1,0:T(1,128)} %bitcast.1, bf16[1024,1024]{1,0:T(8,128)(2,1)} %w_hbm.1), custom_call_target="tpu_custom_call" | custom-call | tf_op jit(solution)/shard_map/pallas_call | solution.py:350
  36.5 1.9 %copy.7 = bf16[256,1024]{1,0:T(8,128)(2,1)} copy(bf16[256,1024]{1,0:T(8,128)(2,1)} %shard_map.55) | data formatting | bytes 1048576
